TPU v7x, 256 devices: a whole 4x4x8 slice. The times are simulated.
256 devices in a mesh: dp: 32 (over z, x_hi, core), tensor: 8 (over y, x_lo).
Axes of the slice: x: 4 (x_hi: 2, x_lo: 2; x = x_hi * 2 + x_lo), y: 4, z: 8, core: 2. Of those that a mesh axis runs over, the one named last changes fastest.
Arguments:
- grads: bfloat16 [32, 40, 128, 4096], P('dp', None, None, 'tensor'), may hold values from -6 to 6
- owner: int32 [40], replicated, may hold values from 0 to 31, as said below
- momentum: float32 [32, 2, 128, 4096], P('dp', None, None, 'tensor'), may hold values from -6 to 6, as said below
Outputs:
- update: bfloat16 [40, 128, 4096], P(None, None, 'tensor')
- new_momentum: float32 [32, 2, 128, 4096], P('dp', None, None, 'tensor')
Inputs may be any that keep to these rules, and one draw needn't show every extreme that they name: Every owner holds at least one matrix and no owner holds more than 2; some owner holds exactly 2. Slot s of owner p holds the momentum of the matrix of slot_rank s among those that owner p holds; slots beyond an owner's count hold values that are carried over.
All inputs are finite; a program needn't handle non-finite values.
Results may differ from a plain program's by a relative error of at most 0.03.
Values may be sent and summed in bfloat16 or wider, within the bound.
A program may use at most 64 MiB of HBM per device.

v0:
```python
import math

import jax
import jax.numpy as jnp
from jax import lax
from jax.sharding import PartitionSpec as P

R = 128
D = 4096
ITERS = 5


COEF_A = 3.4445
COEF_B = -4.775
COEF_C = 2.0315
EPSILON = 1e-07
DECAY = 0.95


def from_everyone(array, axis):
    copies = jnp.broadcast_to(array, (lax.axis_size(axis), *array.shape))
    return lax.all_to_all(copies, axis, split_axis=0, concat_axis=0, tiled=True)


def joined_along(pieces, dim):
    pieces = jnp.moveaxis(pieces, 0, dim)
    shape = pieces.shape
    return pieces.reshape(*shape[:dim], shape[dim] * shape[dim + 1], *shape[dim + 2 :])


def gathered_copies(array, axis, dim):
    pieces = from_everyone(array, axis)
    return joined_along(pieces, dim)


def next_polynomial(gram):
    gram = lax.optimization_barrier(gram)
    square = jnp.einsum("srt,stu->sru", gram, gram, preferred_element_type=jnp.float32)
    return (COEF_B * gram.astype(jnp.float32) + COEF_C * square).astype(jnp.bfloat16)


def apply_polynomial(polynomial, iterate):
    return COEF_A * iterate.astype(jnp.float32) + jnp.einsum(
        "srt,std->srd", polynomial, iterate, preferred_element_type=jnp.float32
    )


def orthogonalize_gathered(rounded, local_cols, factor):
    gathered = gathered_copies(rounded, "tensor", 2)
    squares = jnp.sum(jnp.square(gathered.astype(jnp.float32)), axis=(1, 2))
    iterate = (gathered.astype(jnp.float32) / (jnp.sqrt(squares)[:, None, None] + EPSILON)).astype(
        jnp.bfloat16
    )
    start = lax.axis_index("tensor") * local_cols
    following = None
    for step in range(ITERS):
        gram = jnp.einsum(
            "srd,std->srt", iterate, iterate, preferred_element_type=jnp.float32
        ).astype(jnp.bfloat16)
        polynomial = next_polynomial(gram)
        if step + 1 < ITERS:
            iterate = apply_polynomial(polynomial, iterate).astype(jnp.bfloat16)
        else:
            own_cols = lax.dynamic_slice_in_dim(iterate, start, local_cols, 2)
            following = apply_polynomial(polynomial, own_cols)
    return (factor * following).astype(jnp.bfloat16)


def per_device(grads, owner, momentum):
    owner_count = lax.axis_size("dp")
    myself = lax.axis_index("dp")
    matrices = owner.shape[0]
    slot_count = momentum.shape[1]
    head_rows = grads.shape[2]
    local_cols = grads.shape[3]
    piece_len = head_rows * local_cols // owner_count
    factor = 0.2 * math.sqrt(max(R, D))
    positions = jnp.arange(matrices, dtype=jnp.int32)
    same_owner = owner[:, None] == owner[None, :]
    earlier = positions[None, :] < positions[:, None]
    slot_rank = jnp.sum((same_owner & earlier).astype(jnp.int32), axis=1)
    owner_ids = jnp.arange(owner_count, dtype=jnp.int32)
    slot_ids = jnp.arange(slot_count, dtype=jnp.int32)
    matches = (owner[None, None, :] == owner_ids[:, None, None]) & (
        slot_rank[None, None, :] == slot_ids[None, :, None]
    )
    filled = jnp.any(matches, axis=2)
    source = jnp.sum(jnp.where(matches, positions[None, None, :], 0), axis=2)
    gradient = grads[0]
    zero_float = jnp.zeros((), jnp.float32)
    flattened = gradient.reshape(matrices, head_rows * local_cols).astype(jnp.float32)
    column_part = lax.psum_scatter(
        flattened.astype(jnp.bfloat16), "dp", scatter_dimension=1, tiled=True
    ).astype(jnp.float32)
    outgoing = jnp.take(column_part, source.T.reshape(-1), axis=0).reshape(
        slot_count, owner_count, piece_len
    )
    outgoing = jnp.where(filled.T[:, :, None], outgoing, zero_float)
    incoming = lax.all_to_all(outgoing, "dp", split_axis=1, concat_axis=1, tiled=True)
    mean_grad = incoming.reshape(slot_count, head_rows, local_cols) / owner_count
    previous = momentum[0]
    following = DECAY * previous + mean_grad
    held_here = lax.dynamic_index_in_dim(filled, myself, 0, keepdims=False)
    new_momentum = jnp.where(held_here[:, None, None], following, previous)[None]
    rounded = (mean_grad + DECAY * following).astype(jnp.bfloat16)
    result = orthogonalize_gathered(rounded, local_cols, factor)
    pieces = result.reshape(slot_count, owner_count, piece_len)
    returned = lax.all_to_all(pieces, "dp", split_axis=1, concat_axis=1, tiled=True)
    chosen = jnp.take(
        returned.reshape(slot_count * owner_count, piece_len),
        slot_rank * owner_count + owner,
        axis=0,
    )
    complete = lax.all_gather(chosen, "dp", axis=1, tiled=True)
    update = complete.reshape(matrices, head_rows, local_cols)
    return (update, new_momentum)


def solution(mesh):
    in_specs = (P("dp", None, None, "tensor"), P(), P("dp", None, None, "tensor"))
    out_specs = (P(None, None, "tensor"), P("dp", None, None, "tensor"))
    return jax.shard_map(
        per_device, mesh=mesh, in_specs=in_specs, out_specs=out_specs, check_vma=False
    )
```

profile of v0, /device:TPU:1, one launch (start us, length us, event | category | flops | bytes accessed | tf_op | source)
XLA Modules:
  0.0 357.7 jit_solution(3172155386606064688)
XLA Ops:
  7.2 7.9 %copy.34 = bf16[5,8,128,512]{3,1,2,0:T(8,128)(2,1)} copy(bf16[5,8,128,512]{3,2,1,0:T(8,128)(2,1)} %bitcast.51) | data formatting | bytes 10485760
  16.5 131.4 %reduce-scatter.2.cloned.1.call-done = bf16[40,2048]{1,0:T(8,128)(2,1)} async-done(((bf16[40,65536]{1,0:T(8,128)(2,1)}), bf16[40,2048]{1,0:T(8,128)(2,1)}) %reduce-scatter.2.cloned.1.call-update) | async-done | bytes 163856 | tf_op jit(solution)/shard_map/reduce_scatter | solution.py:92
  147.9 0.9 convert_element_type.104
  148.9 0.8 gather_fusion
  150.3 27.4 %all_to_all.15 = f32[2,32,2048]{2,0,1:T(2,128)S(1)} all-to-all(f32[2,32,2048]{2,0,1:T(2,128)S(1)} %fusion.20), channel_id=1, replica_groups=mesh['dp'=32,'tensor'=8] {'dp'}, dimensions={1} | all-to-all | bytes 1048576 | tf_op jit(solution)/shard_map/all_to_all | solution.py:99
  178.3 1.5 broadcast_in_dim.79
  179.8 4.9 %all-to-all-start.1 = ((bf16[8,2,128,512]{3,2,1,0:T(8,128)(2,1)}), bf16[8,2,128,512]{3,2,1,0:T(8,128)(2,1)S(1)}, u32[]{:S(2)}, u32[]{:S(2)}) async-start(bf16[8,2,128,512]{3,2,1,0:T(8,128)(2,1)} %broadcast_in_dim.79), calls=%async_computation.2 | async-start | bytes 4194304 | tf_op jit(solution)/shard_map/all_to_all | solution.py:22
  184.8 25.7 %all-to-all-done.1 = bf16[8,2,128,512]{3,2,1,0:T(8,128)(2,1)S(1)} async-done(((bf16[8,2,128,512]{3,2,1,0:T(8,128)(2,1)}), bf16[8,2,128,512]{3,2,1,0:T(8,128)(2,1)S(1)}, u32[]{:S(2)}, u32[]{:S(2)}) %all-to-all-start.1) | async-done | bytes 2097184 | tf_op jit(solution)/shard_map/all_to_all | solution.py:22
  213.4 2.2 fusion
  215.7 3.1 convolution_convert_fusion.3
  218.8 2.2 fusion.1
  221.0 3.1 convolution_convert_fusion.2
  224.1 2.2 fusion.2
  226.3 3.1 convolution_convert_fusion.1
  229.4 2.2 fusion.3
  231.6 2.9 convolution_convert_fusion
  234.6 1.4 fusion.6
  236.2 1.0 copy.31
  237.2 7.8 %all-to-all-start.2 = ((bf16[2,32,2048]{2,0,1:T(2,128)(2,1)}), bf16[2,32,2048]{2,0,1:T(2,128)(2,1)S(1)}, u32[]{:S(2)}, u32[]{:S(2)}) async-start(bf16[2,32,2048]{2,0,1:T(2,128)(2,1)} %copy.31), calls=%async_computation.3 | async-start | bytes 524288 | tf_op jit(solution)/shard_map/all_to_all | solution.py:108
  245.1 12.9 %all-to-all-done.2 = bf16[2,32,2048]{2,0,1:T(2,128)(2,1)S(1)} async-done(((bf16[2,32,2048]{2,0,1:T(2,128)(2,1)}), bf16[2,32,2048]{2,0,1:T(2,128)(2,1)S(1)}, u32[]{:S(2)}, u32[]{:S(2)}) %all-to-all-start.2) | async-done | bytes 262176 | tf_op jit(solution)/shard_map/all_to_all | solution.py:108
  258.7 0.8 broadcast_select_fusion
  259.8 1.0 add_select_fusion
  260.8 83.2 %all-gather.2.cloned.1.call-done = bf16[40,65536]{1,0:T(8,128)(2,1)} async-done(((bf16[40,2048]{1,0:T(8,128)(2,1)}), bf16[40,65536]{1,0:T(8,128)(2,1)}) %all-gather.2.cloned.1.call-update) | async-done | bytes 5242896 | tf_op jit(solution)/shard_map/all_gather | solution.py:114
  344.0 6.8 %copy.35 = bf16[5,8,128,512]{3,2,1,0:T(8,128)(2,1)} copy(bf16[5,8,128,512]{3,1,2,0:T(8,128)(2,1)} %bitcast.52) | data formatting | bytes 10485760
  (42 shorter events, 7.0 us)
Async XLA Ops:
  7.2 140.8 %reduce-scatter.2.cloned.1.call-start = ((), (), s32[]{:S(2)}) async-start(), calls=%async_computation.4 | async-start | bytes 5406720 | tf_op jit(solution)/shard_map/reduce_scatter | solution.py:92
  15.1 0.7 copy-start.4
  149.6 28.5 %copy-start.3 = (f32[1,2,128,512]{3,2,1,0:T(8,128)S(1)}, f32[1,2,128,512]{3,2,1,0:T(8,128)}, u32[]{:S(2)}) copy-start(f32[1,2,128,512]{3,2,1,0:T(8,128)} %param.5) | copy-start | bytes 1572868
  179.8 30.6 %all-to-all-start.1 = ((bf16[8,2,128,512]{3,2,1,0:T(8,128)(2,1)}), bf16[8,2,128,512]{3,2,1,0:T(8,128)(2,1)S(1)}, u32[]{:S(2)}, u32[]{:S(2)}) async-start(bf16[8,2,128,512]{3,2,1,0:T(8,128)(2,1)} %broadcast_in_dim.79), calls=%async_computation.2 | async-start | bytes 4194304 | tf_op jit(solution)/shard_map/all_to_all | solution.py:22
  215.7 3.1 copy-start
  221.0 3.1 copy-start.1
  226.3 3.1 copy-start.2
  237.2 20.8 %all-to-all-start.2 = ((bf16[2,32,2048]{2,0,1:T(2,128)(2,1)}), bf16[2,32,2048]{2,0,1:T(2,128)(2,1)S(1)}, u32[]{:S(2)}, u32[]{:S(2)}) async-start(bf16[2,32,2048]{2,0,1:T(2,128)(2,1)} %copy.31), calls=%async_computation.3 | async-start | bytes 524288 | tf_op jit(solution)/shard_map/all_to_all | solution.py:108
  245.0 99.0 %all-gather.2.cloned.1.call-start = ((), (), s32[]{:S(2)}) async-start(), calls=%async_computation.5 | async-start | bytes 5406720 | tf_op jit(solution)/shard_map/all_gather | solution.py:114
Sparse Core Ops, SparseCore 0:
  15.3 132.6 reduce-scatter.1
  259.6 84.3 all-gather.1
where the time goes:
time: 358 us
  waiting for transfers between devices  253 us (71%)
  blocking collectives  27.4 us (8%)
  matrix products  23.2 us (6%)
  local copies, waits for them, and re-layouts  21 us (6%)
  between operations  14.2 us (4%)
  starting transfers between devices  12.9 us (4%)
  other arithmetic  5.8 us (2%)
    reduce_scatter x1, waiting for transfers between devices, per_device(): lax.psum_scatter(flattened.astype(jnp.bfloat16), 'dp', scatter_dimension=...  131 us
    all_gather x1, waiting for transfers between devices, per_device(): complete = lax.all_gather(chosen, 'dp', axis=1, tiled=True)  83.2 us
    all_to_all x1, blocking collectives, per_device(): lax.all_to_all(outgoing, 'dp', split_axis=1, concat_axis=1, tiled=True)  27.4 us
    all_to_all x1, waiting for transfers between devices, from_everyone(): return lax.all_to_all(copies, axis, split_axis=0, concat_axis=0, tiled=True)  25.7 us
    unnamed x12, local copies, waits for them, and re-layouts  15.4 us
    dot_general x5, matrix products, orthogonalize_gathered(): jnp.einsum('srd,std->srt', iterate, iterate, preferred_element_type=jnp.f...  12.9 us
    all_to_all x1, waiting for transfers between devices, per_device(): lax.all_to_all(pieces, 'dp', split_axis=1, concat_axis=1, tiled=True)  12.9 us
    dot_general x5, matrix products, apply_polynomial(): jnp.einsum('srt,std->srd', polynomial, iterate, preferred_element_type=jn...  10.4 us
  transfers between devices with their start and end apart: 4, of which 4 were waited for; matrix products, arithmetic and copies ran while one was open for 1% of the time, Pallas kernels for 0%

commit v1 on v0

v1 whole, which is shorter than its diff:
```python
import functools
import math

import jax
import jax.numpy as jnp
from jax import lax
from jax.experimental import pallas as pl
from jax.experimental.pallas import tpu as pltpu
from jax.sharding import PartitionSpec as P

D = 4096
ITERS = 5
COEF_A = 3.4445
COEF_B = -4.775
COEF_C = 2.0315
EPSILON = 1e-07
DECAY = 0.95

DEPTH = 8
F32 = jnp.float32
BF16 = jnp.bfloat16

GAIN = 1.0 + DECAY

SECOND, HOLDER, PLACE = 32, 40, 48


def table_kernel(owner_ref, out_ref):
    owners = SECOND

    @pl.loop(0, owners)
    def _(p):
        out_ref[p] = -1

    def body(m, count):
        who = owner_ref[m]
        seen = out_ref[who] >= 0

        @pl.when(seen)
        def _():
            out_ref[SECOND + count] = m
            out_ref[HOLDER + count] = who

        @pl.when(jnp.logical_not(seen))
        def _():
            out_ref[who] = m

        out_ref[PLACE + m] = jnp.where(seen, owners + count, who)
        return count + seen.astype(jnp.int32)

    lax.fori_loop(0, owner_ref.shape[0], body, jnp.int32(0))


def order_kernel(place_ref, in_ref, out_ref, held, sems):
    count = out_ref.shape[0]

    def fetch(m):
        return pltpu.make_async_copy(in_ref.at[place_ref[PLACE + m]], held.at[m], sems.at[0, m])

    def store(m):
        return pltpu.make_async_copy(held.at[m], out_ref.at[m], sems.at[1, m])

    for m in range(count):
        fetch(m).start()
    for m in range(count):
        fetch(m).wait()
        store(m).start()
    for m in range(count):
        store(m).wait()


def split(a):
    high = a.astype(BF16)
    return high, (a - high.astype(F32)).astype(BF16)


def dot(a, b):
    return jnp.dot(a, b, preferred_element_type=F32)


def product(a, b):
    return dot(a[0], b[0]) + (dot(a[0], b[1]) + dot(a[1], b[0]))


def polynomials(grams, factor):
    size = grams[0].shape[0]
    row = lax.broadcasted_iota(jnp.int32, (size, size), 0)
    col = lax.broadcasted_iota(jnp.int32, (size, size), 1)
    diagonal = row == col
    eye = jnp.where(diagonal, 1.0, 0.0).astype(F32)
    scales, now = [], []
    for gram in grams:
        total = jnp.sum(jnp.where(diagonal, gram, 0.0), keepdims=True)
        scale = 1.0 / (jnp.sqrt(total) + EPSILON)
        scales.append(scale)
        now.append((gram * scale) * scale)
    totals = [None] * len(grams)
    for step in range(ITERS):
        parts = [split(g) for g in now]
        squares = [product(g, g) for g in parts]
        polys = [COEF_A * eye + COEF_B * g + COEF_C * s for g, s in zip(now, squares)]
        poly_parts = [split(p) for p in polys]
        if step + 1 < ITERS:
            once = [product(p, g) for p, g in zip(poly_parts, parts)]
        if step == 0:
            totals = polys
        else:
            totals = [product(p, split(q)) for p, q in zip(poly_parts, totals)]
        if step + 1 < ITERS:
            now = [product(p, split(o)) for p, o in zip(poly_parts, once)]
    return [q * (scale * factor) for q, scale in zip(totals, scales)]


def step_kernel(
    table, grads, momentum, gathered, new_momentum,
    gv, mv, pstage, precv, xstage, xrecv, zstage, zrecv, tstage, trecv, total, rows16,
    names, gpart, grecv, gsum, gall,
    load_sem, psend, precv_sem, xsend, xrecv_sem, zsend, zrecv_sem, tsend, trecv_sem,
    gsend, grecv_sem, nz, nx, npair, nrecv, az, ax, apair, arecv,
):
    me = lax.axis_index("dp")
    t = lax.axis_index("tensor")
    tensors = lax.axis_size("tensor")
    owners = lax.axis_size("dp")
    c = lax.rem(me, 2)
    h = lax.rem(me // 2, 2)
    z = me // 4
    rows, cols = gv.shape[1], gv.shape[2]
    half = rows // 2
    strip = rows // tensors
    TOP, BOTTOM = pl.ds(0, half), pl.ds(half, half)
    factor = 0.2 * math.sqrt(max(rows, D))
    turn = 1 - 2 * c

    def at(k):
        return lax.rem(z + k + 2 * DEPTH, DEPTH)

    def dp_of(zz, hh, cc):
        return 4 * zz + 2 * hh + cc

    def remote(src, dst, send, recv, dp=None, tensor=None):
        return pltpu.make_async_remote_copy(
            src_ref=src, dst_ref=dst, send_sem=send, recv_sem=recv,
            device_id={"dp": me if dp is None else dp, "tensor": t if tensor is None else tensor},
            device_id_type=pl.DeviceIdType.MESH,
        )

    partner = dp_of(z, h, 1 - c)
    across = dp_of(z, 1 - h, c)
    on0, on1 = c == 0, c == 1
    holder = jnp.logical_and(c == 0, h == 0)

    def toward(k):
        return dp_of(at(k), h, c)

    matrices = gv.shape[0]
    loads = load_sem.shape[0] - 1
    span = matrices // loads
    for i in range(loads):
        pltpu.make_async_copy(
            grads.at[0, pl.ds(i * span, span)], gv.at[pl.ds(i * span, span)], load_sem.at[i]
        ).start()
    pltpu.make_async_copy(momentum.at[0], mv, load_sem.at[loads]).start()

    barrier = pltpu.get_barrier_semaphore()
    for peer in (partner, across, toward(1), toward(-1)):
        pl.semaphore_signal(
            barrier, inc=1, device_id={"dp": peer, "tensor": t}, device_id_type=pl.DeviceIdType.MESH
        )
    for i in range(1, tensors):
        pl.semaphore_signal(
            barrier, inc=1, device_id={"dp": me, "tensor": lax.rem(t + i, tensors)},
            device_id_type=pl.DeviceIdType.MESH,
        )
    pl.semaphore_wait(barrier, 4 + tensors - 1)

    for i in range(loads):
        pltpu.make_async_copy(
            grads.at[0, pl.ds(i * span, span)], gv.at[pl.ds(i * span, span)], load_sem.at[i]
        ).wait()
    pltpu.make_async_copy(momentum.at[0], mv, load_sem.at[loads]).wait()

    order = (4, 3, -3, 2, -2, 1, -1, 0)
    fold = DECAY * DECAY * owners / GAIN

    def extra(zz, part):
        mine = jnp.where(table[HOLDER + zz] == me, fold, 0.0).astype(F32)
        return gv[table[SECOND + zz], part, :].astype(F32) + mine * mv[1, part, :]

    def pair(slot):
        return remote(pstage.at[slot], precv.at[slot], psend.at[slot], precv_sem.at[slot], dp=partner)

    for k in order:
        zz = at(k)
        for hh in range(2):
            pstage[2 * zz + hh] = gv[table[dp_of(zz, hh, 1 - c)]]
            pair(2 * zz + hh).start()

        @pl.when(on1)
        def _():
            for part in (TOP, BOTTOM):
                pstage[16 + zz, part, :] = extra(zz, part).astype(BF16)
            pair(16 + zz).start()

    def own(zz, hh, part):
        return gv[table[dp_of(zz, hh, c)], part, :].astype(F32) + precv[2 * zz + hh, part, :].astype(F32)

    def contribution(u, zz):
        if u == 0:
            return own(zz, h, TOP)
        if u == 1:
            return own(zz, 1 - h, TOP)
        if u == 2:
            return own(zz, h, BOTTOM) + xrecv[zz].astype(F32)
        part = TOP if u == 3 else BOTTOM
        return extra(zz, part) + precv[16 + zz, part, :].astype(F32)

    signs = (1, -1, turn, 1, -1)

    def zcopy(u, slot, src, k):
        return remote(src, zrecv.at[u, slot], zsend.at[u, slot], zrecv_sem.at[u, slot], dp=toward(k))

    def zwait(u, slot):
        zcopy(u, slot, zrecv.at[u, slot], 0 + signs[u]).wait_recv()

    def first(u, place, slot, k, away):
        zstage[u, place] = contribution(u, at(k)).astype(BF16)
        zcopy(u, slot, zstage.at[u, place], away).start()

    def passed(u, slot, k, away):
        zwait(u, slot)
        zrecv[u, slot] = (zrecv[u, slot].astype(F32) + contribution(u, at(k))).astype(BF16)
        zcopy(u, slot + 1, zrecv.at[u, slot], away).start()

    def zstep(u, distance):
        sign = signs[u]
        if distance == 4:
            first(u, 0, 0, 4 * sign, sign)
        elif distance == 3:
            first(u, 1, 4, -3 * sign, -sign)
            passed(u, 0, 3 * sign, sign)
        elif distance == 2:
            passed(u, 1, 2 * sign, sign)
            passed(u, 4, -2 * sign, -sign)
        else:
            passed(u, 2, sign, sign)
            passed(u, 5, -sign, -sign)

    def zlast(u):
        zwait(u, 3)
        zwait(u, 6)
        return contribution(u, z) + (zrecv[u, 3].astype(F32) + zrecv[u, 6].astype(F32))

    def xcopy(zz):
        return remote(xstage.at[zz], xrecv.at[zz], xsend.at[zz], xrecv_sem.at[zz], dp=across)

    def xstep(k):
        zz = at(k)
        for hh in range(2):
            pair(2 * zz + hh).wait_recv()
        xstage[zz] = own(zz, 1 - h, BOTTOM).astype(BF16)
        xcopy(zz).start()

        @pl.when(on0)
        def _():
            pair(16 + zz).wait_recv()

    def group(distance):
        zstep(0, distance)
        zstep(1, distance)

        @pl.when(on0)
        def _():
            zstep(3, distance)
            zstep(4, distance)

    xstep(4)
    zstep(0, 4)
    zstep(1, 4)

    @pl.when(on0)
    def _():
        zstep(3, 4)
        zstep(4, 4)

    for k in order[1:]:
        xstep(k)
    group(3)
    xcopy(at(4)).wait_recv()
    zstep(2, 4)
    group(2)
    for k in (3, -3):
        xcopy(at(k)).wait_recv()
    zstep(2, 3)
    group(1)
    for k in (2, -2):
        xcopy(at(k)).wait_recv()
    zstep(2, 2)

    def tcopy(i):
        return remote(tstage.at[i], trecv.at[i], tsend.at[i], trecv_sem.at[i], dp=across)

    tstage[0] = zlast(1).astype(BF16)
    tcopy(0).start()

    @pl.when(on0)
    def _():
        for i, part in ((1, TOP), (2, BOTTOM)):
            partial = zlast(2 + i)

            @pl.when(h == 1)
            def _():
                tstage[i] = partial.astype(BF16)
                tcopy(i).start()

            @pl.when(h == 0)
            def _():
                total[1, part, :] = partial

    total[0, TOP, :] = zlast(0)
    for k in (1, -1):
        xcopy(at(k)).wait_recv()
    zstep(2, 1)
    xcopy(z).wait_recv()
    total[0, BOTTOM, :] = zlast(2)
    tcopy(0).wait_recv()
    total[0, TOP, :] += trecv[0].astype(F32)

    mean = total[0] * (1.0 / owners)
    following = DECAY * mv[0] + mean
    new_momentum[0, 0] = following
    rows16[0] = (mean + DECAY * following).astype(BF16)

    def gram(j):
        gpart[j] = lax.dot_general(
            rows16[j], rows16[j], (((1,), (1,)), ((), ())), preferred_element_type=F32
        )

    def strip_of(i):
        return pl.ds(pl.multiple_of(i * strip, strip), strip)

    def scatter(j, i, back=False):
        peer = lax.rem(t + i, tensors)
        slot = peer if back else t
        return remote(
            gpart.at[j, strip_of(peer)], grecv.at[j, slot], gsend.at[0, j, i], grecv_sem.at[0, j, slot],
            tensor=peer,
        )

    def spread(j, i, back=False):
        peer = lax.rem(t + i, tensors)
        slot = peer if back else t
        return remote(
            gsum.at[j], gall.at[j, strip_of(slot)], gsend.at[1, j, i], grecv_sem.at[1, j, slot],
            tensor=peer,
        )

    gram(0)
    for i in range(1, tensors):
        scatter(0, i).start()

    def block(ref, zz, u):
        if u == 0:
            return ref.at[dp_of(zz, h, c), TOP], 2 * dp_of(zz, h, c)
        if u == 1:
            return ref.at[dp_of(zz, 1 - h, c), TOP], 2 * dp_of(zz, 1 - h, c)
        if u == 2:
            return ref.at[dp_of(zz, h, c), BOTTOM], 2 * dp_of(zz, h, c) + 1
        base = owners if ref is gathered else 0
        return ref.at[base + zz, TOP if u == 3 else BOTTOM], 2 * (base + zz) + (u - 3)

    def sets(ref):
        return (nz, nx, npair, nrecv) if ref is names else (az, ax, apair, arecv)

    def zhop(ref, u, zz, slot, away):
        z_sem, _, _, recv = sets(ref)
        view, index = block(ref, zz, u)
        return remote(view, view, z_sem.at[u - 3 if ref is names else u, slot], recv.at[index], dp=toward(away))

    def arrival(ref, u, zz):
        z_sem, _, _, recv = sets(ref)
        view, index = block(ref, zz, u)
        return remote(view, view, z_sem.at[0, 0], recv.at[index], dp=across)

    def xhop(ref, view, index, slot):
        _, x_sem, _, recv = sets(ref)
        return remote(view, view, x_sem.at[slot], recv.at[index], dp=across)

    def phop(ref, view, index, slot):
        _, _, p_sem, recv = sets(ref)
        return remote(view, view, p_sem.at[slot], recv.at[index], dp=partner)

    def local(zz, u):
        if u == 0:
            return 4 * zz + 2 * h
        if u == 1:
            return 4 * zz + 2 * (1 - h)
        if u == 2:
            return 4 * zz + 2 * h + 1
        return 32 + 2 * zz + (u - 3)

    def pass_on(ref, u, zz):
        view, index = block(ref, zz, u)
        slot = 2 * zz + u - 3 if ref is names else local(zz, u)
        phop(ref, view, index, slot).start()

    def begin(ref, u):
        sign = signs[u]
        zhop(ref, u, z, 0, sign).start()
        zhop(ref, u, z, 4, -sign).start()
        pass_on(ref, u, z)

    def hop(ref, u, distance):
        sign = signs[u]
        zz = at(-sign * distance)
        arrival(ref, u, zz).wait_recv()
        if distance < 4:
            zhop(ref, u, zz, distance, sign).start()
        pass_on(ref, u, zz)
        done = [zz]
        if distance < 4:
            zz = at(sign * distance)
            arrival(ref, u, zz).wait_recv()
            if distance < 3:
                zhop(ref, u, zz, 4 + distance, -sign).start()
            pass_on(ref, u, zz)
            done.append(zz)
        return done

    @pl.when(holder)
    def _():
        for i, part in ((1, TOP), (2, BOTTOM)):
            tcopy(i).wait_recv()
            value = (total[1, part, :] + trecv[i].astype(F32)) * (GAIN / owners)
            rows16[1, part, :] = value.astype(BF16)
            names[z, part, :] = value.astype(BF16)
        gram(1)
        for i in range(1, tensors):
            scatter(1, i).start()
        for u in (3, 4):
            view, index = block(names, z, u)
            xhop(names, view, index, u - 3).start()
            begin(names, u)

    def reduce_strip(j):
        acc = gpart[j, strip_of(t)]
        for i in range(1, tensors):
            scatter(j, i, back=True).wait_recv()
            acc = acc + grecv[j, lax.rem(t + i, tensors)]
        gsum[j] = acc
        gall[j, strip_of(t)] = acc
        for i in range(1, tensors):
            spread(j, i).start()

    reduce_strip(0)

    @pl.when(holder)
    def _():
        reduce_strip(1)

    @pl.when(jnp.logical_and(on0, h == 1))
    def _():
        for u in (3, 4):
            arrival(names, u, z).wait_recv()
            begin(names, u)

    def finish(js):
        results = polynomials([gall[j] for j in js], factor)
        for j, q in zip(js, results):
            high, low = split(q)
            value = dot(high, rows16[j]) + dot(low, rows16[j])
            gathered[me if j == 0 else owners + z] = value.astype(BF16)

    for i in range(1, tensors):
        spread(0, i, back=True).wait_recv()

    @pl.when(holder)
    def _():
        for i in range(1, tensors):
            spread(1, i, back=True).wait_recv()
        finish((0, 1))

    @pl.when(jnp.logical_not(holder))
    def _():
        finish((0,))

    view, index = block(gathered, z, 0)
    xhop(gathered, view, index, 8).start()
    begin(gathered, 2)
    begin(gathered, 0)
    view, index = block(gathered, z, 2)
    xhop(gathered, view, index, z).start()

    @pl.when(holder)
    def _():
        for u in (3, 4):
            view, index = block(gathered, z, u)
            xhop(gathered, view, index, 6 + u).start()
            begin(gathered, u)

    @pl.when(on0)
    def _():
        for u in (3, 4):
            hop(names, u, 1)

    arrival(gathered, 1, z).wait_recv()
    begin(gathered, 1)

    @pl.when(jnp.logical_and(on0, h == 1))
    def _():
        for u in (3, 4):
            arrival(gathered, u, z).wait_recv()
            begin(gathered, u)

    def from_across(zz):
        index = dp_of(zz, 1 - h, c)
        view = gathered.at[index, BOTTOM]
        xhop(gathered, view, 2 * index + 1, 0).wait_recv()
        phop(gathered, view, 2 * index + 1, 4 * zz + 2 * (1 - h) + 1).start()

    waiting = [z]
    for distance in (1, 2, 3, 4):
        arrived = hop(gathered, 2, distance)
        for zz in arrived:
            view, index = block(gathered, zz, 2)
            xhop(gathered, view, index, zz).start()
        if distance > 1:
            @pl.when(on0)
            def _():
                for u in (3, 4):
                    hop(names, u, distance)
        hop(gathered, 0, distance)
        hop(gathered, 1, distance)

        @pl.when(on0)
        def _():
            for u in (3, 4):
                hop(gathered, u, distance)

        for zz in waiting:
            from_across(zz)
        waiting = arrived
    for zz in waiting:
        from_across(zz)

    def from_partner(ref, view, index):
        phop(ref, view, index, 0).wait_recv()

    @pl.when(on1)
    def _():
        for zz in range(DEPTH):
            for u in (3, 4):
                view, index = block(names, zz, u)
                from_partner(names, view, index)

    has = jnp.float32(0.0)
    which = jnp.int32(0)
    for e in range(DEPTH):
        hit = table[HOLDER + e] == me
        has = jnp.where(hit, 1.0, has)
        which = jnp.where(hit, e, which)
    old = mv[1]
    mean = names[which].astype(F32) * (1.0 / GAIN) - (DECAY * DECAY / GAIN) * old
    new_momentum[0, 1] = old + has * ((DECAY * old + mean) - old)

    for zz in range(DEPTH):
        for hh in range(2):
            for i, part in enumerate((TOP, BOTTOM)):
                index = dp_of(zz, hh, 1 - c)
                from_partner(gathered, gathered.at[index, part], 2 * index + i)

    @pl.when(on1)
    def _():
        for zz in range(DEPTH):
            for u in (3, 4):
                view, index = block(gathered, zz, u)
                from_partner(gathered, view, index)

    for slot in range(16):
        pair(slot).wait_send()
    for zz in range(DEPTH):
        xcopy(zz).wait_send()
    tcopy(0).wait_send()
    for u in range(3):
        for slot in range(7):
            zcopy(u, slot, zrecv.at[u, slot], 1).wait_send()
    for i in range(1, tensors):
        scatter(0, i).wait_send()
        spread(0, i).wait_send()

    def sent(sem):
        view = zrecv.at[0, 0]
        remote(view, view, sem, zrecv_sem.at[0, 0], dp=across).wait_send()

    for u in range(3):
        for slot in range(7):
            sent(az.at[u, slot])
    for i in range(9):
        sent(ax.at[i])
    for i in range(32):
        sent(apair.at[i])

    @pl.when(on1)
    def _():
        for zz in range(DEPTH):
            pair(16 + zz).wait_send()

    @pl.when(on0)
    def _():
        for i in range(2):
            for slot in range(7):
                zcopy(3 + i, slot, zrecv.at[3 + i, slot], 1).wait_send()
                sent(az.at[3 + i, slot])
                sent(nz.at[i, slot])
        for i in range(16):
            sent(apair.at[32 + i])
            sent(npair.at[i])

        @pl.when(h == 1)
        def _():
            for i in (1, 2):
                tcopy(i).wait_send()

    @pl.when(holder)
    def _():
        for i in range(1, tensors):
            scatter(1, i).wait_send()
            spread(1, i).wait_send()
        for i in range(2):
            sent(ax.at[9 + i])
            sent(nx.at[i])


def per_device(grads, owner, momentum):
    tensors = lax.axis_size("tensor")
    matrices, rows, cols = grads.shape[1:]
    slots = momentum.shape[1]
    half = rows // 2
    table = pl.pallas_call(
        table_kernel,
        out_shape=jax.ShapeDtypeStruct((128,), jnp.int32),
        in_specs=[pl.BlockSpec(memory_space=pltpu.SMEM)],
        out_specs=pl.BlockSpec(memory_space=pltpu.SMEM),
        name="tables",
    )(owner)
    dma = pltpu.SemaphoreType.DMA
    gathered, new_momentum = pl.pallas_call(
        step_kernel,
        out_shape=(
            jax.ShapeDtypeStruct((matrices, rows, cols), BF16),
            jax.ShapeDtypeStruct(momentum.shape, F32),
        ),
        in_specs=[
            pl.BlockSpec(memory_space=pltpu.SMEM),
            pl.BlockSpec(memory_space=pl.ANY),
            pl.BlockSpec(memory_space=pl.ANY),
        ],
        out_specs=(
            pl.BlockSpec(memory_space=pltpu.VMEM),
            pl.BlockSpec(memory_space=pltpu.VMEM),
        ),
        scratch_shapes=[
            pltpu.VMEM((matrices, rows, cols), BF16),
            pltpu.VMEM((slots, rows, cols), F32),
            pltpu.VMEM((24, rows, cols), BF16),
            pltpu.VMEM((24, rows, cols), BF16),
            pltpu.VMEM((DEPTH, half, cols), BF16),
            pltpu.VMEM((DEPTH, half, cols), BF16),
            pltpu.VMEM((5, 2, half, cols), BF16),
            pltpu.VMEM((5, 7, half, cols), BF16),
            pltpu.VMEM((3, half, cols), BF16),
            pltpu.VMEM((3, half, cols), BF16),
            pltpu.VMEM((2, rows, cols), F32),
            pltpu.VMEM((2, rows, cols), BF16),
            pltpu.VMEM((DEPTH, rows, cols), BF16),
            pltpu.VMEM((2, rows, rows), F32),
            pltpu.VMEM((2, tensors, rows // tensors, rows), F32),
            pltpu.VMEM((2, rows // tensors, rows), F32),
            pltpu.VMEM((2, rows, rows), F32),
            dma((9,)),
            dma((24,)), dma((24,)),
            dma((DEPTH,)), dma((DEPTH,)),
            dma((5, 7)), dma((5, 7)),
            dma((3,)), dma((3,)),
            dma((2, 2, tensors)), dma((2, 2, tensors)),
            dma((2, 7)), dma((2,)), dma((16,)), dma((16,)),
            dma((5, 7)), dma((11,)), dma((48,)), dma((2 * matrices,)),
        ],
        compiler_params=pltpu.CompilerParams(collective_id=0, has_side_effects=True),
        name="step",
    )(table, grads, momentum)
    update = pl.pallas_call(
        order_kernel,
        out_shape=jax.ShapeDtypeStruct((matrices, rows, cols), BF16),
        in_specs=[
            pl.BlockSpec(memory_space=pltpu.SMEM),
            pl.BlockSpec(memory_space=pl.ANY),
        ],
        out_specs=pl.BlockSpec(memory_space=pl.ANY),
        scratch_shapes=[pltpu.VMEM((matrices, rows, cols), BF16), dma((2, matrices))],
        name="order",
    )(table, gathered)
    return update, new_momentum


def solution(mesh):
    in_specs = (P("dp", None, None, "tensor"), P(), P("dp", None, None, "tensor"))
    out_specs = (P(None, None, "tensor"), P("dp", None, None, "tensor"))
    return jax.shard_map(
        per_device, mesh=mesh, in_specs=in_specs, out_specs=out_specs, check_vma=False
    )
```

time: 358 us -> 93.3 us (0.26)
  waiting for transfers between devices: 253 us -> 0 us
  Pallas kernels: 0 us -> 91.7 us
  blocking collectives: 27.4 us -> 0 us
  matrix products: 23.2 us -> 0 us
  local copies, waits for them, and re-layouts: 21 us -> 0.8 us
  between operations: 14.2 us -> 0.67 us
  starting transfers between devices: 12.9 us -> 0 us
  other arithmetic: 5.8 us -> 0 us
    reduce_scatter x1 -> x0, waiting for transfers between devices: 131 us -> none  [per_device(): lax.psum_scatter(flattened.astype(jnp.bfloat16), 'dp', scatter_dimension=...]
    pallas_call x0 -> x3, Pallas kernels: none -> 91.7 us  [the longest x1 83.7 us: per_device(): pl.pallas_call(step_kernel, out_shape=(jax.ShapeDtypeStruct((matrices, ro...]
    all_gather x1 -> x0, waiting for transfers between devices: 83.2 us -> none  [per_device(): complete = lax.all_gather(chosen, 'dp', axis=1, tiled=True)]
    all_to_all x2 -> x0, waiting for transfers between devices: 38.5 us -> none  [the longest x1 25.7 us: from_everyone(): return lax.all_to_all(copies, axis, split_axis=0, concat_axis=0, tiled=True)]
    all_to_all x1 -> x0, blocking collectives: 27.4 us -> none  [per_device(): lax.all_to_all(outgoing, 'dp', split_axis=1, concat_axis=1, tiled=True)]
    dot_general x10 -> x0, matrix products: 23.2 us -> none  [the longest x5 12.9 us: orthogonalize_gathered(): jnp.einsum('srd,std->srt', iterate, iterate, preferred_element_type=jnp.f...]
    unnamed x12 -> x3, local copies, waits for them, and re-layouts: 15.4 us -> 0.8 us
    all_to_all x2 -> x0, starting transfers between devices: 12.8 us -> none  [the longest x1 7.85 us: per_device(): lax.all_to_all(pieces, 'dp', split_axis=1, concat_axis=1, tiled=True)]
  transfers between devices with their start and end apart: 4 -> 0, of which waited for: 4 -> 0; matrix products, arithmetic and copies ran while one was open for 1% -> 0% of each run, Pallas kernels for 0% -> 0%
where the time goes in v1:
time: 93.3 us; the launch traced here: 93.2 us
  Pallas kernels  91.7 us (98%)
    pallas_call x1, Pallas kernels, per_device(): pl.pallas_call(step_kernel, out_shape=(jax.ShapeDtypeStruct((matrices, ro...  83.7 us
    pallas_call x1, Pallas kernels, per_device(): pl.pallas_call(order_kernel, out_shape=jax.ShapeDtypeStruct((matrices, ro...  6.07 us
    pallas_call x1, Pallas kernels, per_device(): pl.pallas_call(table_kernel, out_shape=jax.ShapeDtypeStruct((128,), jnp.i...  1.96 us

profile of v1, /device:TPU:1, one launch (start us, length us, event | category | flops | bytes accessed | tf_op | source)
XLA Modules:
  0.0 93.2 jit_solution(1292251306584390154)
XLA Ops:
  0.6 2.0 %tables.1.table.place_ref = s32[128]{0:T(128)} custom-call(s32[40]{0:T(128)} %owner_ref.1), custom_call_target="tpu_custom_call" | custom-call | tf_op jit(solution)/shard_map/tables/pallas_call | solution.py:639
  2.6 83.7 %step.1 = (bf16[40,128,512]{2,1,0:T(8,128)(2,1)}, f32[1,2,128,512]{3,2,1,0:T(8,128)}) custom-call(s32[128]{0:T(128)} %tables.1.table.place_ref, bf16[1,40,128,512]{3,2,1,0:T(8,128)(2,1)} %grads.1, f32[1,2,128,512]{3,2,1,0:T(8,128)} %momentum.1), custom_call_target="tpu_custom_call" | custom-call | tf_op jit(solution)/shard_map/step/pallas_call | solution.py:647
  86.3 0.0 copy-start
  86.3 6.1 %order.1 = bf16[40,128,512]{2,1,0:T(8,128)(2,1)} custom-call(s32[128]{0:T(128)} %tables.1.table.place_ref, bf16[40,128,512]{2,1,0:T(8,128)(2,1)} %get-tuple-element.4.in_ref), custom_call_target="tpu_custom_call" | custom-call | tf_op jit(solution)/shard_map/order/pallas_call | solution.py:692
  92.4 0.0 copy-done
  92.4 0.8 copy.6
Async XLA Ops:
  86.3 6.1 %copy-start = (f32[1,2,128,512]{3,2,1,0:T(8,128)S(1)}, f32[1,2,128,512]{3,2,1,0:T(8,128)}, u32[]{:S(2)}) copy-start(f32[1,2,128,512]{3,2,1,0:T(8,128)} %get-tuple-element.9) | copy-start | bytes 1572868

commit v2 on v0

v2 whole, which is shorter than its diff:
```python
import functools
import math

import jax
import jax.numpy as jnp
from jax import lax
from jax.experimental import pallas as pl
from jax.experimental.pallas import tpu as pltpu
from jax.sharding import PartitionSpec as P

D = 4096
ITERS = 5
COEF_A = 3.4445
COEF_B = -4.775
COEF_C = 2.0315
EPSILON = 1e-07
DECAY = 0.95

DEPTH = 8
F32 = jnp.float32
BF16 = jnp.bfloat16

GAIN = 1.0 + DECAY

FIRST, SECOND, HOLDER, PLACE = range(4)


def tables(owner, owners, out):
    count = owner.shape[1]

    def grid(shape, dim):
        return lax.broadcasted_iota(jnp.int32, shape, dim)

    def column(row):
        size = row.shape[1]
        square = (size, size)
        kept = jnp.where(grid(square, 0) == grid(square, 1), jnp.broadcast_to(row, square), 0)
        return jnp.sum(kept, axis=1, keepdims=True)

    held = column(owner) == grid((count, owners), 1)
    which = grid((count, owners), 0)
    first = jnp.min(jnp.where(held, which, count - 1), axis=0, keepdims=True)
    last = jnp.max(jnp.where(held, which, -1), axis=0, keepdims=True)
    first_c, last_c = column(first), column(last)
    two = jnp.where(last > first, 1, 0)
    two_c = column(two)
    square = (owners, owners)
    rank = jnp.sum(
        jnp.where(grid(square, 0) < grid(square, 1), jnp.broadcast_to(two_c, square), 0),
        axis=0, keepdims=True,
    )
    rank_c = column(rank)
    eighth = (owners, DEPTH)
    chosen = jnp.logical_and(
        jnp.broadcast_to(rank_c, eighth) == grid(eighth, 1), jnp.broadcast_to(two_c, eighth) > 0
    )
    second = jnp.sum(jnp.where(chosen, jnp.broadcast_to(last_c, eighth), 0), axis=0, keepdims=True)
    holder = jnp.sum(jnp.where(chosen, grid(eighth, 0), 0), axis=0, keepdims=True)
    wide = (owners, count)
    spot = jnp.where(
        jnp.broadcast_to(first_c, wide) == grid(wide, 1), grid(wide, 0), owners + rank_c
    )
    place = jnp.sum(
        jnp.where(jnp.broadcast_to(owner, wide) == grid(wide, 0), spot, 0), axis=0, keepdims=True
    )
    out[FIRST, 0:owners] = first[0]
    out[SECOND, 0:DEPTH] = second[0]
    out[HOLDER, 0:DEPTH] = holder[0]
    out[PLACE, 0:count] = place[0]


def order_kernel(table, in_ref, momentum, out_ref, out_momentum, sems):
    count = out_ref.shape[0]

    def copy(m):
        return pltpu.make_async_copy(in_ref.at[table[PLACE, m]], out_ref.at[m], sems.at[m])

    rest = pltpu.make_async_copy(momentum, out_momentum, sems.at[count])
    for m in range(count):
        copy(m).start()
    rest.start()
    for m in range(count):
        copy(m).wait()
    rest.wait()


def split(a):
    high = a.astype(BF16)
    return high, (a - high.astype(F32)).astype(BF16)


def dot(a, b):
    return jnp.dot(a, b, preferred_element_type=F32)


def product(a, b):
    return dot(a[0], b[0]) + (dot(a[0], b[1]) + dot(a[1], b[0]))


def polynomials(grams, factor):
    size = grams[0].shape[0]
    row = lax.broadcasted_iota(jnp.int32, (size, size), 0)
    col = lax.broadcasted_iota(jnp.int32, (size, size), 1)
    diagonal = row == col
    eye = jnp.where(diagonal, 1.0, 0.0).astype(F32)
    scales, now = [], []
    for gram in grams:
        total = jnp.sum(jnp.where(diagonal, gram, 0.0), keepdims=True)
        scale = 1.0 / (jnp.sqrt(total) + EPSILON)
        scales.append(scale)
        now.append((gram * scale) * scale)
    totals = [None] * len(grams)
    for step in range(ITERS):
        parts = [split(g) for g in now]
        squares = [product(g, g) for g in parts]
        polys = [COEF_A * eye + COEF_B * g + COEF_C * s for g, s in zip(now, squares)]
        poly_parts = [split(p) for p in polys]
        if step + 1 < ITERS:
            once = [product(p, g) for p, g in zip(poly_parts, parts)]
        if step == 0:
            totals = polys
        else:
            totals = [product(p, split(q)) for p, q in zip(poly_parts, totals)]
        if step + 1 < ITERS:
            now = [product(p, split(o)) for p, o in zip(poly_parts, once)]
    return [q * (scale * factor) for q, scale in zip(totals, scales)]


def step_kernel(
    owner, grads, momentum, gathered, new_momentum, table_out,
    gv, mv, pstage, precv, xstage, xrecv, zstage, zrecv, tstage, trecv, total,
    nall, qall, gpart, grecv, gsum, gall, table, folded,
    load_sem, sent, precv_sem, xrecv_sem, zrecv_sem, trecv_sem, grecv_sem,
    arecv, parecv, qrecv, pqrecv,
):
    (s_pair, s_x, s_z, s_top, s_az, s_xtop, s_xbottom, s_xextra, s_passed, s_qz, s_qze, s_qx, s_qxe,
     s_qpassed) = (sent.at[i] for i in range(14))
    s_scatter, s_spread = (sent.at[14], sent.at[16]), (sent.at[15], sent.at[17])
    me = lax.axis_index("dp")
    t = lax.axis_index("tensor")
    tensors = lax.axis_size("tensor")
    owners = lax.axis_size("dp")
    c = lax.rem(me, 2)
    h = lax.rem(me // 2, 2)
    z = me // 4
    rows, cols = gv.shape[1], gv.shape[2]
    half = rows // 2
    strip = rows // tensors
    TOP, BOTTOM = pl.ds(0, half), pl.ds(half, half)
    factor = 0.2 * math.sqrt(max(rows, D))
    turn = 1 - 2 * c

    def at(k):
        return lax.rem(z + k + 2 * DEPTH, DEPTH)

    def dp_of(zz, hh, cc):
        return 4 * zz + 2 * hh + cc

    def remote(src, dst, send, recv, dp=None, tensor=None):
        return pltpu.make_async_remote_copy(
            src_ref=src, dst_ref=dst, send_sem=send, recv_sem=recv,
            device_id={"dp": me if dp is None else dp, "tensor": t if tensor is None else tensor},
            device_id_type=pl.DeviceIdType.MESH,
        )

    partner = dp_of(z, h, 1 - c)
    across = dp_of(z, 1 - h, c)
    on0, on1 = c == 0, c == 1
    holder = jnp.logical_and(c == 0, h == 0)

    def toward(k):
        return dp_of(at(k), h, c)
    matrices = gv.shape[0]
    loads = 8
    span = matrices // loads
    for i in range(loads):
        pltpu.make_async_copy(
            grads.at[0, pl.ds(i * span, span)], gv.at[pl.ds(i * span, span)], load_sem.at[0]
        ).start()
    momentum_load = pltpu.make_async_copy(momentum.at[0], mv, load_sem.at[1])
    momentum_load.start()

    barrier = pltpu.get_barrier_semaphore()
    for peer in (partner, across, toward(1), toward(-1)):
        pl.semaphore_signal(
            barrier, inc=1, device_id={"dp": peer, "tensor": t}, device_id_type=pl.DeviceIdType.MESH
        )
    for i in range(1, tensors):
        pl.semaphore_signal(
            barrier, inc=1, device_id={"dp": me, "tensor": lax.rem(t + i, tensors)},
            device_id_type=pl.DeviceIdType.MESH,
        )

    table_out[...] = jnp.zeros_like(table_out)
    tables(owner[...], owners, table_out)
    to_scalars = pltpu.make_async_copy(table_out, table, load_sem.at[2])
    to_scalars.start()
    pl.semaphore_wait(barrier, 4 + tensors - 1)
    momentum_load.wait()
    folded[...] = (mv[1] * (DECAY * DECAY * owners / GAIN)).astype(BF16)
    to_scalars.wait()
    pltpu.make_async_copy(grads.at[0], gv, load_sem.at[0]).wait()

    order = (4, 3, -3, 2, -2, 1, -1, 0)

    def chosen(row, i):
        return jnp.clip(table[row, i], 0, matrices - 1)

    def extra(zz, part):
        mine = jnp.where(table[HOLDER, zz] == me, 1.0, 0.0).astype(BF16)
        return gv[chosen(SECOND, zz), part, :] + mine * folded[part, :]

    def pair(slot, zz):
        return remote(pstage.at[slot], precv.at[slot], s_pair, precv_sem.at[zz], dp=partner)
    for k in order:
        zz = at(k)
        for hh in range(2):
            pstage[2 * zz + hh] = gv[chosen(FIRST, dp_of(zz, hh, 1 - c))]
            pair(2 * zz + hh, zz).start()

        @pl.when(on1)
        def _():
            for part in (TOP, BOTTOM):
                pstage[16 + zz, part, :] = extra(zz, part)
            pair(16 + zz, zz).start()

    def several(ref, send, recv, dp=partner):
        return remote(ref, ref, send, recv, dp=dp)

    def paired(*offsets):
        for k in offsets:
            for here, matrices in ((on0, 3), (on1, 2)):
                @pl.when(here)
                def _():
                    several(precv.at[pl.ds(0, matrices)], s_pair, precv_sem.at[at(k)]).wait_recv()

    def own(zz, hh, part):
        return gv[chosen(FIRST, dp_of(zz, hh, c)), part, :] + precv[2 * zz + hh, part, :]

    def contribution(u, zz):
        if u == 0:
            return own(zz, h, TOP)
        if u == 1:
            return own(zz, 1 - h, TOP)
        if u == 2:
            return own(zz, h, BOTTOM) + xrecv[zz]
        part = TOP if u == 3 else BOTTOM
        return extra(zz, part) + precv[16 + zz, part, :]

    signs = (1, -1, turn, 1, -1)

    def zcopy(u, slot, src, k):
        return remote(src, zrecv.at[u, slot], s_z, zrecv_sem.at[u, slot], dp=toward(k))

    def zwait(u, slot):
        zcopy(u, slot, zrecv.at[u, slot], signs[u]).wait_recv()

    def first(u, place, slot, k, away):
        zstage[u, place] = contribution(u, at(k))
        zcopy(u, slot, zstage.at[u, place], away).start()

    def passed(u, slot, k, away):
        zwait(u, slot)
        zrecv[u, slot] = zrecv[u, slot] + contribution(u, at(k))
        zcopy(u, slot + 1, zrecv.at[u, slot], away).start()

    def z4(u):
        first(u, 0, 0, 4 * signs[u], signs[u])

    def z3b(u):
        first(u, 1, 4, -3 * signs[u], -signs[u])

    def z3a(u):
        passed(u, 0, 3 * signs[u], signs[u])

    def z3(u):
        z3b(u)
        z3a(u)

    def z2(u):
        passed(u, 1, 2 * signs[u], signs[u])
        passed(u, 4, -2 * signs[u], -signs[u])

    def z1(u):
        passed(u, 2, signs[u], signs[u])
        passed(u, 5, -signs[u], -signs[u])

    def zlast(u):
        zwait(u, 3)
        zwait(u, 6)
        return contribution(u, z).astype(F32) + (zrecv[u, 3].astype(F32) + zrecv[u, 6].astype(F32))

    def xcopy(zz):
        return remote(xstage.at[zz], xrecv.at[zz], s_x, xrecv_sem.at[zz], dp=across)

    def xstep(*offsets):
        for k in offsets:
            zz = at(k)
            xstage[zz] = own(zz, 1 - h, BOTTOM)
            xcopy(zz).start()

    def crossed(*offsets):
        for k in offsets:
            xcopy(at(k)).wait_recv()

    def every(step):
        step(0)
        step(1)

        @pl.when(on0)
        def _():
            step(3)
            step(4)
    paired(4)
    every(z4)
    xstep(4)
    paired(3, -3)
    every(z3b)
    xstep(3, -3)
    every(z3a)
    paired(2, -2)
    xstep(2, -2)
    paired(1, -1)
    xstep(1, -1)
    crossed(4)
    z4(2)
    every(z2)
    paired(0)
    xstep(0)
    crossed(3, -3)
    z3(2)
    every(z1)
    crossed(2, -2)
    z2(2)

    def tcopy(i):
        return remote(
            tstage.at[i], trecv.at[i], s_top, trecv_sem.at[0 if i == 0 else 1], dp=across
        )
    tstage[0] = zlast(1).astype(BF16)
    tcopy(0).start()

    @pl.when(on0)
    def _():
        for i, part in ((1, TOP), (2, BOTTOM)):
            partial = zlast(2 + i)

            @pl.when(h == 1)
            def _():
                tstage[i] = partial.astype(BF16)
                tcopy(i).start()

            @pl.when(h == 0)
            def _():
                total[1, part, :] = partial

    total[0, TOP, :] = zlast(0)
    crossed(1, -1)
    z1(2)

    def block(zz, u):
        if u < 3:
            hh = 1 - h if u == 1 else h
            lower = 1 if u == 2 else 0
            return nall.at[dp_of(zz, hh, c), BOTTOM if lower else TOP], 4 * zz + 2 * hh + lower
        return nall.at[owners + zz, TOP if u == 3 else BOTTOM], 4 * DEPTH + 2 * zz + (u - 3)

    def zhop(u, zz, away):
        view, index = block(zz, u)
        return remote(view, view, s_az, arecv.at[index], dp=toward(away))

    def xhop(zz, u, send):
        view, index = block(zz, u)
        return remote(view, view, send, arecv.at[index], dp=across)

    def phop(view, zz):
        return remote(view, view, s_passed, parecv.at[zz], dp=partner)

    def arrived(u, zz):
        xhop(zz, u, s_az).wait_recv()

    def pass_on(u, zz):
        phop(block(zz, u)[0], zz).start()

    def begin(u):
        zhop(u, z, signs[u]).start()
        zhop(u, z, -signs[u]).start()

    def hop(u, distance):
        for side, far in ((signs[u], 4), (-signs[u], 3)):
            if distance > far:
                continue
            zz = at(-side * distance)
            arrived(u, zz)
            if distance < far:
                zhop(u, zz, side).start()
            if u == 2:
                xhop(zz, 2, s_xbottom).start()
            pass_on(u, zz)

    def across_block(zz):
        return nall.at[dp_of(zz, 1 - h, c), BOTTOM], 4 * zz + 2 * (1 - h) + 1

    def from_across(zz):
        view, index = across_block(zz)
        remote(view, view, s_xbottom, arecv.at[index], dp=across).wait_recv()
        phop(view, zz).start()

    def nesterov(part):
        mean = total[0, part, :] * (1.0 / owners)
        following = DECAY * mv[0, part, :] + mean
        new_momentum[0, 0, part, :] = following
        nall[me, part, :] = (mean + DECAY * following).astype(BF16)
    crossed(0)
    total[0, BOTTOM, :] = zlast(2)
    nesterov(BOTTOM)
    begin(2)
    tcopy(0).wait_recv()
    total[0, TOP, :] += trecv[0].astype(F32)
    nesterov(TOP)
    xhop(z, 0, s_xtop).start()
    begin(0)
    xhop(z, 2, s_xbottom).start()

    def strip_of(i):
        return pl.ds(pl.multiple_of(i * strip, strip), strip)

    def scatter(j, i):
        peer = lax.rem(t + i, tensors)
        return remote(
            gpart.at[j, strip_of(peer)], grecv.at[j, t], s_scatter[j], grecv_sem.at[0, j], tensor=peer
        )

    def spread(j, i):
        peer = lax.rem(t + i, tensors)
        return remote(
            gsum.at[j], gall.at[j, strip_of(t)], s_spread[j], grecv_sem.at[1, j], tensor=peer
        )

    def strips(j, phase):
        view = grecv.at[j, pl.ds(0, tensors - 1)]
        return several(view, (s_spread if phase else s_scatter)[j], grecv_sem.at[phase, j])

    def gram(j, value):
        gpart[j] = lax.dot_general(
            value, value, (((1,), (1,)), ((), ())), preferred_element_type=F32
        )
        for i in range(1, tensors):
            scatter(j, i).start()
    gram(0, nall[me])
    pass_on(2, z)
    pass_on(0, z)

    @pl.when(holder)
    def _():
        several(trecv.at[pl.ds(1, 2)], s_top, trecv_sem.at[1]).wait_recv()
        for i, part in ((1, TOP), (2, BOTTOM)):
            value = (total[1, part, :] + trecv[i].astype(F32)) * (GAIN / owners)
            nall[owners + z, part, :] = value.astype(BF16)
        gram(1, nall[owners + z])
        for u in (3, 4):
            xhop(z, u, s_xextra).start()
            begin(u)
            pass_on(u, z)
    arrived(1, z)
    begin(1)
    pass_on(1, z)

    def reduce_strip(j):
        strips(j, 0).wait_recv()
        acc = gpart[j, strip_of(t)]
        for i in range(1, tensors):
            acc = acc + grecv[j, lax.rem(t + i, tensors)]
        gsum[j] = acc
        gall[j, strip_of(t)] = acc
        for i in range(1, tensors):
            spread(j, i).start()
    reduce_strip(0)

    @pl.when(holder)
    def _():
        reduce_strip(1)
    @pl.when(jnp.logical_and(on0, h == 1))
    def _():
        for u in (3, 4):
            arrived(u, z)
            begin(u)
            pass_on(u, z)

    def gather_step(distance, units=(2, 0, 1)):
        for u in units:
            hop(u, distance)

    def gather_extra(distance):
        @pl.when(on0)
        def _():
            for u in (3, 4):
                hop(u, distance)
    gather_step(1, (2, 0))

    def qhop_to(zz, hh, extra, send, dp):
        index = owners + zz if extra else dp_of(zz, hh, c)
        mine = 2 * DEPTH + zz if extra else 2 * zz + hh
        return remote(qall.at[index], qall.at[index], send, qrecv.at[mine], dp=dp)

    def qzhop(zz, away, extra):
        return qhop_to(zz, h, extra, s_qze if extra else s_qz, toward(away))

    def qxhop(zz, hh, extra):
        return qhop_to(zz, hh, extra, s_qxe if extra else s_qx, across)

    def qphop(zz, hh, extra):
        index = owners + zz if extra else dp_of(zz, hh, c)
        return remote(qall.at[index], qall.at[index], s_qpassed, pqrecv.at[zz], dp=partner)

    qsigns = (turn, 1)

    def qbegin(extra):
        sign = qsigns[1 if extra else 0]
        qzhop(z, sign, extra).start()
        qzhop(z, -sign, extra).start()
        qxhop(z, h, extra).start()
        qphop(z, h, extra).start()

    def qhop(distance, extra=False):
        sign = qsigns[1 if extra else 0]
        for side, far in ((sign, 4), (-sign, 3)):
            if distance > far:
                continue
            zz = at(-side * distance)
            qxhop(zz, h, extra).wait_recv()
            if distance < far:
                qzhop(zz, side, extra).start()
            qxhop(zz, h, extra).start()
            qphop(zz, h, extra).start()

    def qacross(zz):
        qxhop(zz, 1 - h, False).wait_recv()
        qphop(zz, 1 - h, False).start()

        @pl.when(jnp.logical_and(on0, h == 1))
        def _():
            qxhop(zz, 0, True).wait_recv()
            qphop(zz, 0, True).start()

    def qstep(distance):
        qhop(distance)

        @pl.when(holder)
        def _():
            qhop(distance, True)

    def finish(js):
        results = polynomials([gall[j] for j in js], factor)
        for j, q in zip(js, results):
            qall[me if j == 0 else owners + z] = q.astype(BF16)
            qbegin(j == 1)
    strips(0, 1).wait_recv()
    @pl.when(holder)
    def _():
        strips(1, 1).wait_recv()
        finish((0, 1))

    @pl.when(jnp.logical_not(holder))
    def _():
        finish((0,))

    def both(distance):
        return (z,) if distance == 0 else (at(4),) if distance == 4 else (at(distance), at(-distance))

    def multiply(index):
        gathered[index] = dot(qall[index], nall[index]).astype(BF16)

    def apply(zz):
        for here, count in ((on0, 2), (on1, 3)):
            @pl.when(here)
            def _():
                several(nall.at[pl.ds(0, count)], s_passed, parecv.at[zz]).wait_recv()
                several(qall.at[pl.ds(0, count)], s_qpassed, pqrecv.at[zz]).wait_recv()

        @pl.loop(0, 2)
        def _(i):
            multiply(4 * zz + 2 * i)
            multiply(4 * zz + 2 * i + 1)

        multiply(owners + zz)

    def crossing(distance):
        for zz in both(distance):
            from_across(zz)

    def qcrossing(distance):
        for zz in both(distance):
            qacross(zz)
    gather_step(1, (1,))
    gather_extra(1)
    gather_step(2)
    gather_extra(2)
    crossing(0)
    crossing(1)
    qstep(1)
    qcrossing(0)
    gather_step(3)
    gather_extra(3)
    qstep(2)
    crossing(2)
    qcrossing(1)
    gather_step(4)
    gather_extra(4)
    qstep(3)
    crossing(3)
    qcrossing(2)
    apply(z)
    qstep(4)
    crossing(4)
    qcrossing(3)
    for zz in both(1):
        apply(zz)
    qcrossing(4)
    for zz in both(2):
        apply(zz)
    for zz in both(3):
        apply(zz)
    apply(at(4))
    has = jnp.float32(0.0)
    which = jnp.int32(0)
    for e in range(DEPTH):
        hit = table[HOLDER, e] == me
        has = jnp.where(hit, 1.0, has)
        which = jnp.where(hit, e, which)
    old = mv[1]
    mean = nall[owners + which].astype(F32) * (1.0 / GAIN) - (DECAY * DECAY / GAIN) * old
    new_momentum[0, 1] = old + has * ((DECAY * old + mean) - old)
    def left(ref, send):
        remote(ref, ref, send, zrecv_sem.at[0, 0], dp=across).wait_send()

    left(xstage, s_x)
    left(xstage, s_xbottom)
    left(xstage.at[0], s_xtop)
    left(qall.at[pl.ds(0, 7)], s_qz)
    left(qall.at[pl.ds(0, DEPTH)], s_qx)
    strips(0, 0).wait_send()
    strips(0, 1).wait_send()

    @pl.when(on1)
    def _():
        left(pstage, s_pair)
        left(zrecv.at[pl.ds(0, 3)], s_z)
        left(zrecv.at[pl.ds(0, 3)], s_az)
        left(tstage.at[0], s_top)
        left(nall.at[pl.ds(0, 16)], s_passed)
        left(qall.at[pl.ds(0, 16)], s_qpassed)

    @pl.when(on0)
    def _():
        left(pstage.at[pl.ds(0, 16)], s_pair)
        left(zrecv, s_z)
        left(zrecv, s_az)
        left(nall.at[pl.ds(0, 24)], s_passed)
        left(qall.at[pl.ds(0, 24)], s_qpassed)

        @pl.when(h == 1)
        def _():
            left(tstage, s_top)

        @pl.when(h == 0)
        def _():
            left(tstage.at[0], s_top)

    @pl.when(holder)
    def _():
        strips(1, 0).wait_send()
        strips(1, 1).wait_send()
        left(xstage.at[pl.ds(0, 2)], s_xextra)
        left(qall.at[pl.ds(0, 7)], s_qze)
        left(qall.at[pl.ds(0, DEPTH)], s_qxe)
def per_device(grads, owner, momentum):
    tensors = lax.axis_size("tensor")
    matrices, rows, cols = grads.shape[1:]
    slots = momentum.shape[1]
    half = rows // 2
    dma = pltpu.SemaphoreType.DMA
    whole = pl.BlockSpec(memory_space=pltpu.VMEM)
    far = pl.BlockSpec(memory_space=pltpu.HBM)
    gathered, new_momentum, table = pl.pallas_call(
        step_kernel,
        out_shape=(
            jax.ShapeDtypeStruct((matrices, rows, cols), BF16),
            jax.ShapeDtypeStruct(momentum.shape, F32),
            jax.ShapeDtypeStruct((8, 128), jnp.int32),
        ),
        in_specs=[whole, far, far],
        out_specs=(whole, whole, whole),
        scratch_shapes=[
            pltpu.VMEM((matrices, rows, cols), BF16),
            pltpu.VMEM((slots, rows, cols), F32),
            pltpu.VMEM((24, rows, cols), BF16),
            pltpu.VMEM((24, rows, cols), BF16),
            pltpu.VMEM((DEPTH, half, cols), BF16),
            pltpu.VMEM((DEPTH, half, cols), BF16),
            pltpu.VMEM((5, 2, half, cols), BF16),
            pltpu.VMEM((5, 7, half, cols), BF16),
            pltpu.VMEM((3, half, cols), BF16),
            pltpu.VMEM((3, half, cols), BF16),
            pltpu.VMEM((2, rows, cols), F32),
            pltpu.VMEM((matrices, rows, cols), BF16),
            pltpu.VMEM((matrices, rows, rows), BF16),
            pltpu.VMEM((2, rows, rows), F32),
            pltpu.VMEM((2, tensors, rows // tensors, rows), F32),
            pltpu.VMEM((2, rows // tensors, rows), F32),
            pltpu.VMEM((2, rows, rows), F32),
            pltpu.SMEM((8, 128), jnp.int32),
            pltpu.VMEM((rows, cols), BF16),
            dma((3,)), dma((18,)), dma((DEPTH,)), dma((DEPTH,)), dma((5, 7)), dma((2,)), dma((2, 2)),
            dma((6 * DEPTH,)), dma((DEPTH,)), dma((3 * DEPTH,)), dma((DEPTH,)),
        ],
        compiler_params=pltpu.CompilerParams(
            collective_id=0, has_side_effects=True, vmem_limit_bytes=46 * 2**20
        ),
        name="step",
    )(owner.reshape(1, matrices), grads, momentum)
    return pl.pallas_call(
        order_kernel,
        out_shape=(
            jax.ShapeDtypeStruct((matrices, rows, cols), BF16),
            jax.ShapeDtypeStruct(momentum.shape, F32),
        ),
        in_specs=[
            pl.BlockSpec(memory_space=pltpu.SMEM),
            pl.BlockSpec(memory_space=pl.ANY),
            pl.BlockSpec(memory_space=pl.ANY),
        ],
        out_specs=(far, far),
        scratch_shapes=[dma((matrices + 1,))],
        compiler_params=pltpu.CompilerParams(vmem_limit_bytes=2**20),
        name="order",
    )(table, gathered, new_momentum)


def solution(mesh):
    in_specs = (P("dp", None, None, "tensor"), P(), P("dp", None, None, "tensor"))
    out_specs = (P(None, None, "tensor"), P("dp", None, None, "tensor"))
    return jax.shard_map(
        per_device, mesh=mesh, in_specs=in_specs, out_specs=out_specs, check_vma=False
    )
```

time: 358 us -> 80.4 us (0.22)
  waiting for transfers between devices: 253 us -> 0 us
  Pallas kernels: 0 us -> 77.9 us
  blocking collectives: 27.4 us -> 0 us
  matrix products: 23.2 us -> 0 us
  local copies, waits for them, and re-layouts: 21 us -> 1.69 us
  between operations: 14.2 us -> 0.65 us
  starting transfers between devices: 12.9 us -> 0 us
  other arithmetic: 5.8 us -> 0 us
    reduce_scatter x1 -> x0, waiting for transfers between devices: 131 us -> none  [per_device(): lax.psum_scatter(flattened.astype(jnp.bfloat16), 'dp', scatter_dimension=...]
    all_gather x1 -> x0, waiting for transfers between devices: 83.2 us -> none  [per_device(): complete = lax.all_gather(chosen, 'dp', axis=1, tiled=True)]
    pallas_call x0 -> x2, Pallas kernels: none -> 77.9 us  [the longest x1 74.5 us: per_device(): pl.pallas_call(step_kernel, out_shape=(jax.ShapeDtypeStruct((matrices, ro...]
    all_to_all x2 -> x0, waiting for transfers between devices: 38.5 us -> none  [the longest x1 25.7 us: from_everyone(): return lax.all_to_all(copies, axis, split_axis=0, concat_axis=0, tiled=True)]
    all_to_all x1 -> x0, blocking collectives: 27.4 us -> none  [per_device(): lax.all_to_all(outgoing, 'dp', split_axis=1, concat_axis=1, tiled=True)]
    dot_general x10 -> x0, matrix products: 23.2 us -> none  [the longest x5 12.9 us: orthogonalize_gathered(): jnp.einsum('srd,std->srt', iterate, iterate, preferred_element_type=jnp.f...]
    unnamed x12 -> x4, local copies, waits for them, and re-layouts: 15.4 us -> 1.69 us
    all_to_all x2 -> x0, starting transfers between devices: 12.8 us -> none  [the longest x1 7.85 us: per_device(): lax.all_to_all(pieces, 'dp', split_axis=1, concat_axis=1, tiled=True)]
  transfers between devices with their start and end apart: 4 -> 0, of which waited for: 4 -> 0; matrix products, arithmetic and copies ran while one was open for 1% -> 0% of each run, Pallas kernels for 0% -> 0%
where the time goes in v2:
time: 80.4 us; the launch traced here: 80.3 us
  Pallas kernels  77.9 us (97%)
  local copies, waits for them, and re-layouts  1.69 us (2%)
    pallas_call x1, Pallas kernels, per_device(): pl.pallas_call(step_kernel, out_shape=(jax.ShapeDtypeStruct((matrices, ro...  74.5 us
    pallas_call x1, Pallas kernels, per_device(): pl.pallas_call(order_kernel, out_shape=(jax.ShapeDtypeStruct((matrices, r...  3.44 us
    unnamed x4, local copies, waits for them, and re-layouts  1.69 us

profile of v2, /device:TPU:1, one launch (start us, length us, event | category | flops | bytes accessed | tf_op | source)
XLA Modules:
  0.0 80.3 jit_solution(1847322960151330519)
XLA Ops:
  0.6 0.0 copy-start
  0.6 1.0 %copy-done = f32[1,2,128,512]{3,2,1,0:T(8,128)S(1)} copy-done((f32[1,2,128,512]{3,2,1,0:T(8,128)S(1)}, f32[1,2,128,512]{3,2,1,0:T(8,128)}, u32[]{:S(2)}) %copy-start) | copy-done | bytes 524312
  1.7 0.0 copy-start.1
  1.7 0.7 copy-done.1
  2.3 74.5 %step.1 = (bf16[40,128,512]{2,1,0:T(8,128)(2,1)S(1)}, f32[1,2,128,512]{3,2,1,0:T(8,128)S(1)}, s32[8,128]{1,0:T(8,128)S(1)}) custom-call(s32[1,40]{1,0:T(1,128)S(1)} %bitcast.1, bf16[1,40,128,512]{3,2,1,0:T(8,128)(2,1)} %grads.1, f32[1,2,128,512]{3,2,1,0:T(8,128)S(1)} %copy-done), custom_call_target="tpu_custom_call" | custom-call | tf_op jit(solution)/shard_map/step/pallas_call | solution.py:685
  76.8 3.4 %order.1 = (bf16[40,128,512]{2,1,0:T(8,128)(2,1)}, f32[1,2,128,512]{3,2,1,0:T(8,128)}) custom-call(s32[8,128]{1,0:T(8,128)S(1)} %get-tuple-element.5.table, bf16[40,128,512]{2,1,0:T(8,128)(2,1)S(1)} %get-tuple-element.6.in_ref, f32[1,2,128,512]{3,2,1,0:T(8,128)S(1)} %get-tuple-element.7.momentum), custom_call_target="tpu_custom_call" | custom-call | tf_op jit(solution)/shard_map/order/pallas_call | solution.py:722
Async XLA Ops:
  0.6 1.0 %copy-start = (f32[1,2,128,512]{3,2,1,0:T(8,128)S(1)}, f32[1,2,128,512]{3,2,1,0:T(8,128)}, u32[]{:S(2)}) copy-start(f32[1,2,128,512]{3,2,1,0:T(8,128)} %momentum.1) | copy-start | bytes 1572868
  1.7 0.7 copy-start.1

commit v3 on v2

--- a/solution.py
+++ b/solution.py
@@ -127,9 +127,9 @@
 
 
 def step_kernel(
-    owner, grads, momentum, gathered, new_momentum, table_out,
+    owner_in, grads, momentum, gathered, new_momentum, table_out,
     gv, mv, pstage, precv, xstage, xrecv, zstage, zrecv, tstage, trecv, total,
-    nall, qall, gpart, grecv, gsum, gall, table, folded,
+    nall, qall, gpart, grecv, gsum, gall, table, folded, owner,
     load_sem, sent, precv_sem, xrecv_sem, zrecv_sem, trecv_sem, grecv_sem,
     arecv, parecv, qrecv, pqrecv,
 ):
@@ -171,6 +171,8 @@
     def toward(k):
         return dp_of(at(k), h, c)
     matrices = gv.shape[0]
+    owner_load = pltpu.make_async_copy(owner_in, owner, load_sem.at[3])
+    owner_load.start()
     loads = 8
     span = matrices // loads
     for i in range(loads):
@@ -191,6 +193,7 @@
             device_id_type=pl.DeviceIdType.MESH,
         )
 
+    owner_load.wait()
     table_out[...] = jnp.zeros_like(table_out)
     tables(owner[...], owners, table_out)
     to_scalars = pltpu.make_async_copy(table_out, table, load_sem.at[2])
@@ -329,9 +332,17 @@
     xstep(0)
     crossed(3, -3)
     z3(2)
-    every(z1)
+    z1(1)
+
+    @pl.when(on0)
+    def _():
+        z1(3)
+        z1(4)
     crossed(2, -2)
     z2(2)
+    z1(0)
+    crossed(1, -1)
+    z1(2)
 
     def tcopy(i):
         return remote(
@@ -355,8 +366,6 @@
                 total[1, part, :] = partial
 
     total[0, TOP, :] = zlast(0)
-    crossed(1, -1)
-    z1(2)
 
     def block(zz, u):
         if u < 3:
@@ -594,31 +603,35 @@
             qacross(zz)
     gather_step(1, (1,))
     gather_extra(1)
-    gather_step(2)
-    gather_extra(2)
+    hop(2, 2)
     crossing(0)
     crossing(1)
     qstep(1)
+    gather_step(2, (0, 1))
     qcrossing(0)
-    gather_step(3)
+    gather_extra(2)
+    qstep(2)
+    qcrossing(1)
+    hop(2, 3)
+    hop(0, 3)
+    crossing(2)
+    qstep(3)
+    hop(1, 3)
     gather_extra(3)
-    qstep(2)
-    crossing(2)
-    qcrossing(1)
-    gather_step(4)
-    gather_extra(4)
-    qstep(3)
+    apply(z)
+    hop(2, 4)
     crossing(3)
     qcrossing(2)
-    apply(z)
     qstep(4)
+    gather_step(4, (0, 1))
+    gather_extra(4)
+    for zz in both(1):
+        apply(zz)
     crossing(4)
     qcrossing(3)
-    for zz in both(1):
+    for zz in both(2):
         apply(zz)
     qcrossing(4)
-    for zz in both(2):
-        apply(zz)
     for zz in both(3):
         apply(zz)
     apply(at(4))
@@ -689,7 +702,7 @@
             jax.ShapeDtypeStruct(momentum.shape, F32),
             jax.ShapeDtypeStruct((8, 128), jnp.int32),
         ),
-        in_specs=[whole, far, far],
+        in_specs=[far, far, far],
         out_specs=(whole, whole, whole),
         scratch_shapes=[
             pltpu.VMEM((matrices, rows, cols), BF16),
@@ -711,14 +724,15 @@
             pltpu.VMEM((2, rows, rows), F32),
             pltpu.SMEM((8, 128), jnp.int32),
             pltpu.VMEM((rows, cols), BF16),
-            dma((3,)), dma((18,)), dma((DEPTH,)), dma((DEPTH,)), dma((5, 7)), dma((2,)), dma((2, 2)),
+            pltpu.VMEM((1, matrices), jnp.int32),
+            dma((4,)), dma((18,)), dma((DEPTH,)), dma((DEPTH,)), dma((5, 7)), dma((2,)), dma((2, 2)),
             dma((6 * DEPTH,)), dma((DEPTH,)), dma((3 * DEPTH,)), dma((DEPTH,)),
         ],
         compiler_params=pltpu.CompilerParams(
             collective_id=0, has_side_effects=True, vmem_limit_bytes=46 * 2**20
         ),
         name="step",
-    )(owner.reshape(1, matrices), grads, momentum)
+    )(*(pltpu.with_memory_space_constraint(a, pltpu.HBM) for a in (owner.reshape(1, matrices), grads, momentum)))
     return pl.pallas_call(
         order_kernel,
         out_shape=(

time: 80.4 us -> 75.3 us (0.937)
  Pallas kernels: 77.9 us -> 74.6 us
  local copies, waits for them, and re-layouts: 1.69 us -> 0 us
    pallas_call x1, Pallas kernels: 74.5 us -> 71.1 us  [per_device(): pl.pallas_call(step_kernel, out_shape=(jax.ShapeDtypeStruct((matrices, ro...]
    unnamed x4 -> x0, local copies, waits for them, and re-layouts: 1.69 us -> none
where the time goes in v3:
time: 75.3 us; the launch traced here: 75.2 us
  Pallas kernels  74.6 us (99%)
    pallas_call x1, Pallas kernels, per_device(): pl.pallas_call(step_kernel, out_shape=(jax.ShapeDtypeStruct((matrices, ro...  71.1 us
    pallas_call x1, Pallas kernels, per_device(): pl.pallas_call(order_kernel, out_shape=(jax.ShapeDtypeStruct((matrices, r...  3.44 us

profile of v3, /device:TPU:1, one launch (start us, length us, event | category | flops | bytes accessed | tf_op | source)
XLA Modules:
  0.0 75.2 jit_solution(12429332091302113856)
XLA Ops:
  0.6 71.1 %step.1 = (bf16[40,128,512]{2,1,0:T(8,128)(2,1)S(1)}, f32[1,2,128,512]{3,2,1,0:T(8,128)S(1)}, s32[8,128]{1,0:T(8,128)S(1)}) custom-call(s32[1,40]{1,0:T(1,128)} %bitcast.1, bf16[1,40,128,512]{3,2,1,0:T(8,128)(2,1)} %grads.1, f32[1,2,128,512]{3,2,1,0:T(8,128)} %momentum.1), custom_call_target="tpu_custom_call" | custom-call | tf_op jit(solution)/shard_map/step/pallas_call | solution.py:698
  71.8 3.4 %order.1 = (bf16[40,128,512]{2,1,0:T(8,128)(2,1)}, f32[1,2,128,512]{3,2,1,0:T(8,128)}) custom-call(s32[8,128]{1,0:T(8,128)S(1)} %get-tuple-element.5.table, bf16[40,128,512]{2,1,0:T(8,128)(2,1)S(1)} %get-tuple-element.6.in_ref, f32[1,2,128,512]{3,2,1,0:T(8,128)S(1)} %get-tuple-element.7.momentum), custom_call_target="tpu_custom_call" | custom-call | tf_op jit(solution)/shard_map/order/pallas_call | solution.py:736

commit v4 on v3

--- a/solution.py
+++ b/solution.py
@@ -94,7 +94,7 @@
 
 
 def product(a, b):
-    return dot(a[0], b[0]) + (dot(a[0], b[1]) + dot(a[1], b[0]))
+    return dot(jnp.concatenate([a[0], a[1], a[0]], axis=1), jnp.concatenate([b[0], b[0], b[1]], axis=0))
 
 
 def polynomials(grams, factor):
@@ -587,11 +587,8 @@
                 several(nall.at[pl.ds(0, count)], s_passed, parecv.at[zz]).wait_recv()
                 several(qall.at[pl.ds(0, count)], s_qpassed, pqrecv.at[zz]).wait_recv()
 
-        @pl.loop(0, 2)
-        def _(i):
-            multiply(4 * zz + 2 * i)
-            multiply(4 * zz + 2 * i + 1)
-
+        for i in range(4):
+            multiply(4 * zz + i)
         multiply(owners + zz)
 
     def crossing(distance):
@@ -623,10 +620,10 @@
     crossing(3)
     qcrossing(2)
     qstep(4)
+    for zz in both(1):
+        apply(zz)
     gather_step(4, (0, 1))
     gather_extra(4)
-    for zz in both(1):
-        apply(zz)
     crossing(4)
     qcrossing(3)
     for zz in both(2):

time: 75.3 us -> 74.2 us (0.985)
  Pallas kernels: 74.6 us -> 73.5 us
    pallas_call x1, Pallas kernels: 71.1 us -> 70 us  [per_device(): pl.pallas_call(step_kernel, out_shape=(jax.ShapeDtypeStruct((matrices, ro...]
where the time goes in v4:
time: 74.2 us; the launch traced here: 74.1 us
  Pallas kernels  73.5 us (99%)
    pallas_call x1, Pallas kernels, per_device(): pl.pallas_call(step_kernel, out_shape=(jax.ShapeDtypeStruct((matrices, ro...  70 us
    pallas_call x1, Pallas kernels, per_device(): pl.pallas_call(order_kernel, out_shape=(jax.ShapeDtypeStruct((matrices, r...  3.44 us

profile of v4, /device:TPU:1, one launch (start us, length us, event | category | flops | bytes accessed | tf_op | source)
XLA Modules:
  0.0 74.1 jit_solution(11716155540633666104)
XLA Ops:
  0.6 70.0 %step.1 = (bf16[40,128,512]{2,1,0:T(8,128)(2,1)S(1)}, f32[1,2,128,512]{3,2,1,0:T(8,128)S(1)}, s32[8,128]{1,0:T(8,128)S(1)}) custom-call(s32[1,40]{1,0:T(1,128)} %bitcast.1, bf16[1,40,128,512]{3,2,1,0:T(8,128)(2,1)} %grads.1, f32[1,2,128,512]{3,2,1,0:T(8,128)} %momentum.1), custom_call_target="tpu_custom_call" | custom-call | tf_op jit(solution)/shard_map/step/pallas_call | solution.py:695
  70.7 3.4 %order.1 = (bf16[40,128,512]{2,1,0:T(8,128)(2,1)}, f32[1,2,128,512]{3,2,1,0:T(8,128)}) custom-call(s32[8,128]{1,0:T(8,128)S(1)} %get-tuple-element.5.table, bf16[40,128,512]{2,1,0:T(8,128)(2,1)S(1)} %get-tuple-element.6.in_ref, f32[1,2,128,512]{3,2,1,0:T(8,128)S(1)} %get-tuple-element.7.momentum), custom_call_target="tpu_custom_call" | custom-call | tf_op jit(solution)/shard_map/order/pallas_call | solution.py:733
